TPU v7x, 32 devices: a whole 2x2x4 slice. The times are simulated.
32 devices in a mesh: pb: 8 (over y, x, core), pa: 4 (over z).
Axes of the slice: x: 2, y: 2, z: 4, core: 2. Of those that a mesh axis runs over, the one named last changes fastest.
Arguments:
- queries: bfloat16 [2048, 128], P('pb'), may hold values from -10.5 to 10.5, as said below
- encoder_outputs: bfloat16 [8, 64, 128, 1024], P('pb', 'pa'), may hold values from -6 to 6
- proj_weight: bfloat16 [1024, 128], replicated, may hold values from -0.1875 to 0.1875
- bm25_rank: int32 [64, 4, 64], P('pb', 'pa'), may hold values from 0 to 199
- dense_rank: int32 [64, 4, 64], P('pb', 'pa'), may hold values from 0 to 199
- custodian_document_index: int32 [8, 64], P('pb', 'pa'), may hold values from -1 to 31, as said below
Outputs:
- query_grad: float32 [2048, 128], P(('pb', 'pa'))
- encoder_output_derivative: bfloat16 [8, 64, 128, 1024], P('pb', 'pa')
Inputs may be any that keep to these rules, and one draw needn't show every extreme that they name: `queries`: A custom draw: each entry lies between the bounds; rows may differ in scale. `custodian_document_index`: within each row b every number n from 0 to 31 appears exactly once and stands for passage (n // 8, b * 8 + n % 8); all other entries are -1. The owner of columns o * 16 to o * 16 + 15 is index o of pa; an owner holds 0, 8 or 16 passages, and at most 4 with the same n // 8. Some owner is full and some owner holds exactly 4 passages with the same n // 8 in every row.
All inputs are finite; a program needn't handle non-finite values.
Results may differ from a plain program's by a relative error of at most 0.025.
The roundings to bfloat16 on the way count: a program that leaves them out, or rounds other values in their place, can miss the bound.
Values may be sent and summed in bfloat16 or wider, within the bound.
A program may use at most 64 MiB of HBM per device.

v0:
```python
import jax
import jax.numpy as jnp
from jax import lax
from jax.sharding import PartitionSpec as P

DIM = 128
H = 1024
QT = 32
LEN = 128
PD = 8
DEPTH = 100
CAP = 16
tau = 0.05
inv_temp = 20.0
rrf_offset = 60.0
norm_eps = 1e-06


def normalize(hid_rows, weight):
    projected = jnp.dot(hid_rows, weight, preferred_element_type=jnp.float32)
    scaling = lax.rsqrt(jnp.sum(projected * projected, axis=-1, keepdims=True) + norm_eps)
    return (projected * scaling, scaling)


def joined_target(bm25_rank, dense_rank):
    first = jnp.where(
        bm25_rank < DEPTH, rrf_offset / (rrf_offset + bm25_rank.astype(jnp.float32)), 0.0
    )
    second = jnp.where(
        dense_rank < DEPTH, rrf_offset / (rrf_offset + dense_rank.astype(jnp.float32)), 0.0
    )
    return first + second


def routing(slot_ids, width_pa, sendable):
    filled = slot_ids >= 0
    destination = jnp.where(filled, slot_ids // PD, -1)
    positions = jnp.arange(CAP, dtype=jnp.int32)
    earlier = (destination[None, :] == destination[:, None]) & (
        positions[None, :] < positions[:, None]
    )
    rank_in = jnp.sum(earlier.astype(jnp.int32), axis=1)
    target_at = jnp.where(filled, destination * sendable + rank_in, width_pa * sendable)
    flat_index = jnp.arange(width_pa * sendable, dtype=jnp.int32)
    matches = target_at[None, :] == flat_index[:, None]
    present = jnp.any(matches, axis=1)
    source = jnp.sum(jnp.where(matches, positions[None, :], 0), axis=1)
    labels = jnp.sum(jnp.where(matches, slot_ids[None, :] % PD, 0), axis=1)
    labels = jnp.where(present, labels, -1)
    return (filled, target_at, source, present, labels)


def pick_rows(table, index_list, keep):
    picked = jnp.take(table, jnp.clip(index_list, 0, table.shape[0] - 1), axis=0)
    keep_shape = keep.reshape(keep.shape + (1,) * (picked.ndim - 1))
    return jnp.where(keep_shape, picked, jnp.zeros((), picked.dtype))


def arrival_index(labels):
    wanted = jnp.arange(PD, dtype=jnp.int32)
    matches = labels[None, :] == wanted[:, None]
    slot_numbers = jnp.arange(labels.shape[0], dtype=jnp.int32)
    return jnp.sum(jnp.where(matches, slot_numbers[None, :], 0), axis=1)


def similarity(query_rows, key_block):
    shards = key_block.shape[0]
    flat_keys = key_block.reshape(shards * LEN, key_block.shape[-1])
    raw = (
        jnp.einsum("rd,kd->rk", query_rows, flat_keys, preferred_element_type=jnp.float32)
        * inv_temp
    )
    return raw.reshape(query_rows.shape[0], shards, LEN)


def log_total(raw):
    largest = jnp.max(raw, axis=2, keepdims=True)
    return largest[:, :, 0] + jnp.log(jnp.sum(jnp.exp(raw - largest), axis=2))


def on_device(
    queries, encoder_outputs, proj_weight, bm25_rank, dense_rank, custodian_document_index
):
    width_pa = lax.axis_size("pa")
    sendable = (2 * PD + width_pa - 1) // width_pa
    query_rows = queries.shape[0]
    query_count = query_rows // QT
    passages_all = bm25_rank.shape[2]
    zero_index = jnp.int32(0)
    hid_slots = encoder_outputs[0]
    slot_ids = custodian_document_index[0]
    filled, target_at, source, present, labels = routing(slot_ids, width_pa, sendable)
    unit_rows, scaling = normalize(hid_slots.reshape(CAP * LEN, H), proj_weight)
    emb_slots = unit_rows.astype(jnp.bfloat16).reshape(CAP, LEN, DIM)
    outgoing = pick_rows(emb_slots, source, present).reshape(width_pa, sendable, LEN, DIM)
    arrived, arrived_labels = (
        lax.all_to_all(outgoing, "pa", split_axis=0, concat_axis=0, tiled=True),
        lax.all_to_all(
            labels.reshape(width_pa, sendable), "pa", split_axis=0, concat_axis=0, tiled=True
        ),
    )
    arrived_flat = arrived.reshape(width_pa * sendable, LEN, DIM)
    label_flat = arrived_labels.reshape(width_pa * sendable)
    local_emb = jnp.take(arrived_flat, arrival_index(label_flat), axis=0)
    lse_start = jnp.zeros((query_rows, passages_all), jnp.float32)
    forward_start = (lse_start,)
    key_pieces = lax.all_gather(local_emb, "pb", axis=0, tiled=True)
    begin_at = jnp.int32(0)
    shards = key_pieces.shape[0] // PD

    def forward_one_shard(turn, state):
        key_block = lax.dynamic_slice_in_dim(key_pieces, turn * PD, PD, 0)
        sums = log_total(similarity(queries, key_block))
        return lax.dynamic_update_slice(state, sums, (zero_index, turn * PD))

    lse_part = lax.fori_loop(0, shards, forward_one_shard, forward_start[0])
    kept_parts = tuple(
        (
            lax.dynamic_update_slice_in_dim(kept, key_pieces, begin_at, 0)
            for kept in forward_start[1:]
        )
    )
    forward_state = (lse_part,) + kept_parts
    lse_all = forward_state[0]
    score = lse_all.reshape(query_count, QT, passages_all).sum(axis=1) * (tau / QT)
    residual = (score - joined_target(bm25_rank[:, 0, :], dense_rank[:, 0, :])).astype(jnp.bfloat16)
    residual_rows = jnp.repeat(residual, QT, axis=0)
    residual_wide = residual_rows.astype(jnp.float32)
    start_state = (
        jnp.zeros((query_rows, DIM), jnp.float32),
        jnp.zeros((passages_all * LEN, DIM), jnp.float32),
    )
    backward_key_pieces = lax.all_gather(local_emb, "pb", axis=0, tiled=True)
    shards = backward_key_pieces.shape[0] // PD

    def backward_one_shard(turn, state):
        query_acc, emb_acc = state
        offset = turn * PD
        key_block = lax.dynamic_slice_in_dim(backward_key_pieces, turn * PD, PD, 0)
        raw = similarity(queries, key_block)
        log_sums = lax.dynamic_slice_in_dim(lse_all, offset, PD, 1)
        weights = jnp.exp(raw - log_sums[:, :, None])
        residual_cols = lax.dynamic_slice_in_dim(residual_wide, offset, PD, 1)
        coefficient = (
            ((residual_cols / QT)[:, :, None] * weights)
            .astype(jnp.bfloat16)
            .reshape(query_rows, PD * LEN)
        )
        query_acc = query_acc + jnp.dot(
            coefficient, key_block.reshape(PD * LEN, DIM), preferred_element_type=jnp.float32
        )
        emb_part = jnp.einsum("rk,rd->kd", coefficient, queries, preferred_element_type=jnp.float32)
        emb_acc = lax.dynamic_update_slice(emb_acc, emb_part, (offset * LEN, zero_index))
        return (query_acc, emb_acc)

    query_acc, emb_acc = lax.fori_loop(0, shards, backward_one_shard, start_state)
    query_grad = lax.psum_scatter(
        query_acc.astype(jnp.bfloat16), "pa", scatter_dimension=0, tiled=True
    ).astype(jnp.float32)
    emb_grad = lax.psum_scatter(
        emb_acc.astype(jnp.bfloat16), "pb", scatter_dimension=0, tiled=True
    ).reshape(PD, LEN, DIM)
    keep_back = label_flat >= 0
    returning = pick_rows(emb_grad, label_flat, keep_back).reshape(width_pa, sendable, LEN, DIM)
    came_back = lax.all_to_all(returning, "pa", split_axis=0, concat_axis=0, tiled=True).reshape(
        width_pa * sendable, LEN, DIM
    )
    slot_grad = pick_rows(came_back, target_at, filled).astype(jnp.float32).reshape(CAP * LEN, DIM)
    inner = jnp.sum(unit_rows * slot_grad, axis=-1, keepdims=True)
    slot_proj_grad = ((slot_grad - unit_rows * inner) * scaling).astype(jnp.bfloat16)
    hid_grad = jnp.einsum(
        "rd,hd->rh", slot_proj_grad, proj_weight, preferred_element_type=jnp.float32
    )
    encoder_output_derivative = hid_grad.astype(jnp.bfloat16).reshape(1, CAP, LEN, H)
    return (query_grad, encoder_output_derivative)


def solution(mesh):
    return jax.shard_map(
        on_device,
        mesh=mesh,
        in_specs=(
            P("pb", None),
            P("pb", "pa", None, None),
            P(),
            P("pb", "pa", None),
            P("pb", "pa", None),
            P("pb", "pa"),
        ),
        out_specs=(P(("pb", "pa"), None), P("pb", "pa", None, None)),
        check_vma=False,
    )
```

profile of v0, /device:TPU:0, one launch (start us, length us, event | category | flops | bytes accessed | tf_op | source)
XLA Modules:
  0.0 195.5 jit_solution(11533505428949204612)
XLA Ops:
  7.2 0.7 fusion.34
  7.9 0.7 fusion.22
  8.7 0.7 fusion.18
  9.6 0.7 select_n.172
  10.3 6.3 %all-to-all-start = ((s32[4,1,4]{2,1,0:T(1,128)}), s32[4,1,4]{2,1,0:T(1,128)S(1)}, u32[]{:S(2)}, u32[]{:S(2)}) async-start(s32[4,1,4]{2,1,0:T(1,128)} %bitcast.9), calls=%async_computation | async-start | bytes 4096 | tf_op jit(solution)/shard_map/all_to_all | solution.py:98
  16.7 3.5 %multiply_reduce_fusion = (f32[2048]{0:T(1024)S(1)}, f32[2048,128]{1,0:T(8,128)S(1)}) fusion(bf16[2048,1024]{1,0:T(8,128)(2,1)} %bitcast.128, bf16[1024,128]{1,0:T(8,128)(2,1)S(1)} %copy-done), kind=kOutput, calls=%fused_computation.31 | convolution fusion | flops 537393152 | bytes 5513216 | tf_op jit(solution)/shard_map/dot_general | solution.py:20
  20.2 0.9 copy-done.1
  21.6 0.6 gather_fusion.2
  22.2 0.9 select_select_fusion.1
  23.2 5.1 %all-to-all-start.1 = ((bf16[4,4,128,128]{3,2,1,0:T(8,128)(2,1)}), bf16[4,4,128,128]{3,2,1,0:T(8,128)(2,1)S(1)}, u32[]{:S(2)}, u32[]{:S(2)}) async-start(bf16[4,4,128,128]{3,2,1,0:T(8,128)(2,1)} %bitcast.12), calls=%async_computation.1 | async-start | bytes 1048576 | tf_op jit(solution)/shard_map/all_to_all | solution.py:97
  28.3 0.5 broadcast.369
  28.8 0.7 fusion.23
  29.7 12.5 %all-to-all-done.1 = bf16[4,4,128,128]{3,2,1,0:T(8,128)(2,1)S(1)} async-done(((bf16[4,4,128,128]{3,2,1,0:T(8,128)(2,1)}), bf16[4,4,128,128]{3,2,1,0:T(8,128)(2,1)S(1)}, u32[]{:S(2)}, u32[]{:S(2)}) %all-to-all-start.1) | async-done | bytes 524320 | tf_op jit(solution)/shard_map/all_to_all | solution.py:97
  42.2 0.6 gather_fusion
  42.8 0.8 broadcast_select_fusion
  43.7 26.9 %all-gather.2.cloned.1.call-done = bf16[64,128,128]{2,1,0:T(8,128)(2,1)} async-done(((bf16[8,128,128]{2,1,0:T(8,128)(2,1)}), bf16[64,128,128]{2,1,0:T(8,128)(2,1)}) %all-gather.2.cloned.1.call-update) | async-done | bytes 2097168 | tf_op jit(solution)/shard_map/all_gather | solution.py:133
  70.7 11.9 %while.31 = (s32[]{:T(128)}, f32[256,64]{0,1:T(8,128)S(1)}, bf16[64,128,128]{2,1,0:T(8,128)(2,1)}, bf16[256,128]{1,0:T(8,128)(2,1)S(1)}, s32[]{:T(128)}, /*index=5*/s32[]{:T(128)}, s32[]{:T(128)}, s32[]{:T(128)}) while((s32[]{:T(128)}, f32[256,64]{0,1:T(8,128)S(1)}, bf16[64,128,128]{2,1,0:T(8,128)(2,1)}, bf16[256,128]{1,0:T(8,128)(2,1)S(1)}, ...), condition=%wide.region_9.11_spmd, body=%wide.region_6.10_spmd.sunk | while | flops 68155400 | bytes 2998419 | solution.py:116
  70.7 1.0 constant_dynamic-slice_fusion.5
  72.2 1.0 constant_dynamic-slice_fusion.5
  73.7 1.0 constant_dynamic-slice_fusion.5
  75.1 1.0 constant_dynamic-slice_fusion.5
  76.6 1.0 constant_dynamic-slice_fusion.5
  78.1 1.0 constant_dynamic-slice_fusion.5
  79.6 1.0 constant_dynamic-slice_fusion.5
  81.1 1.0 constant_dynamic-slice_fusion.5
  82.8 1.5 broadcast_in_dim.131
  84.3 27.7 %while.32 = (s32[]{:T(128)}, f32[256,128]{1,0:T(8,128)S(1)}, bf16[8192,128]{1,0:T(8,128)(2,1)}, f32[256,64]{0,1:T(8,128)S(1)}, bf16[64,128,128]{2,1,0:T(8,128)(2...) while((s32[]{:T(128)}, f32[256,128]{1,0:T(8,128)S(1)}, ...), condition=%wide.region_12.14_spmd.clone, body=%wide.region_11.13_spmd.clone.sunk | while | flops 203229184 | bytes 7274743 | solution.py:156
  84.3 1.0 constant_dynamic-slice_fusion.6
  86.0 0.7 fusion.54
  86.7 1.0 convolution_dynamic-update-slice_fusion.2
  87.7 1.0 constant_dynamic-slice_fusion.6
  89.4 0.7 fusion.54
  90.2 1.0 convolution_dynamic-update-slice_fusion.2
  91.2 1.0 constant_dynamic-slice_fusion.6
  92.2 0.4 fusion.53
  92.9 0.7 fusion.54
  93.7 1.0 convolution_dynamic-update-slice_fusion.2
  94.7 1.0 constant_dynamic-slice_fusion.6
  95.7 0.4 fusion.53
  96.4 0.7 fusion.54
  97.1 1.0 convolution_dynamic-update-slice_fusion.2
  98.1 1.0 constant_dynamic-slice_fusion.6
  99.1 0.4 fusion.53
  99.8 0.7 fusion.54
  100.6 1.0 convolution_dynamic-update-slice_fusion.2
  101.6 1.0 constant_dynamic-slice_fusion.6
  103.3 0.7 fusion.54
  104.0 1.0 convolution_dynamic-update-slice_fusion.2
  105.1 1.0 constant_dynamic-slice_fusion.6
  106.8 0.7 fusion.54
  107.5 1.0 convolution_dynamic-update-slice_fusion.2
  108.5 1.0 constant_dynamic-slice_fusion.6
  110.2 0.7 fusion.54
  111.0 1.0 convolution_dynamic-update-slice_fusion.2
  112.2 41.1 %reduce-scatter.5.cloned.1.call-done = bf16[1024,128]{1,0:T(8,128)(2,1)} async-done(((bf16[8192,128]{1,0:T(8,128)(2,1)}), bf16[1024,128]{1,0:T(8,128)(2,1)}) %reduce-scatter.5.cloned.1.call-update) | async-done | bytes 262160 | tf_op jit(solution)/shard_map/reduce_scatter | solution.py:160
  153.2 1.6 gather_fusion.1
  154.9 0.9 select_select_fusion.2
  155.8 4.6 %all-to-all-start.2 = ((bf16[4,4,128,128]{3,2,1,0:T(8,128)(2,1)}), bf16[4,4,128,128]{3,2,1,0:T(8,128)(2,1)S(1)}, u32[]{:S(2)}, u32[]{:S(2)}) async-start(bf16[4,4,128,128]{3,2,1,0:T(8,128)(2,1)} %select_select_fusion.2), calls=%async_computation.4 | async-start | bytes 1048576 | tf_op jit(solution)/shard_map/all_to_all | solution.py:165
  160.4 0.6 convert_element_type.65
  161.2 22.1 %reduce-scatter.3.cloned.1.call-done = bf16[64,128]{1,0:T(8,128)(2,1)} async-done(((bf16[256,128]{1,0:T(8,128)(2,1)}), bf16[64,128]{1,0:T(8,128)(2,1)}) %reduce-scatter.3.cloned.1.call-update) | async-done | bytes 16400 | tf_op jit(solution)/shard_map/reduce_scatter | solution.py:157
  183.3 1.3 convert_element_type.66
  184.6 0.6 gather_fusion.3
  185.4 0.7 fusion.8
  186.1 2.9 %convolution_convert_fusion = bf16[2048,1024]{1,0:T(8,128)(2,1)} fusion(bf16[1024,128]{1,0:T(8,128)(2,1)S(1)} %copy-done, bf16[2048,128]{1,0:T(8,128)(2,1)S(1)} %bitcast.129, f32[2048,128]{1,0:T(8,128)S(1)} %copy-done.2, f32[2048]{0:T(1024)S(1)} %fusion.8, f32[2048]{0:T(1024)S(1)} %add_rsqrt_fusion), kind=kOutput, calls=%fused_computation.25 | convolution fusion | flops 540540928 | bytes 6045696 | tf_op jit(solution)/shard_map/rd,hd->rh/dot_general | solution.py:171
  (96 shorter events, 10.0 us)
Async XLA Ops:
  7.2 9.5 %copy-start = (bf16[1024,128]{1,0:T(8,128)(2,1)S(1)}, bf16[1024,128]{1,0:T(8,128)(2,1)}, u32[]{:S(2)}) copy-start(bf16[1024,128]{1,0:T(8,128)(2,1)} %param.14) | copy-start | bytes 786436
  10.3 12.8 %all-to-all-start = ((s32[4,1,4]{2,1,0:T(1,128)}), s32[4,1,4]{2,1,0:T(1,128)S(1)}, u32[]{:S(2)}, u32[]{:S(2)}) async-start(s32[4,1,4]{2,1,0:T(1,128)} %bitcast.9), calls=%async_computation | async-start | bytes 4096 | tf_op jit(solution)/shard_map/all_to_all | solution.py:98
  20.2 1.0 copy-start.1
  21.5 22.1 %copy-start.4 = (s32[8,1,64]{2,1,0:T(1,128)S(1)}, s32[8,1,64]{2,1,0:T(1,128)}, u32[]{:S(2)}) copy-start(s32[8,1,64]{2,1,0:T(1,128)} %param.15) | copy-start | bytes 6148
  21.5 22.1 %copy-start.5 = (s32[8,1,64]{2,1,0:T(1,128)S(1)}, s32[8,1,64]{2,1,0:T(1,128)}, u32[]{:S(2)}) copy-start(s32[8,1,64]{2,1,0:T(1,128)} %param.16) | copy-start | bytes 6148
  21.5 49.1 %copy-start.3 = (bf16[256,128]{1,0:T(8,128)(2,1)S(1)}, bf16[256,128]{1,0:T(8,128)(2,1)}, u32[]{:S(2)}) copy-start(bf16[256,128]{1,0:T(8,128)(2,1)} %param.12) | copy-start | bytes 196612
  23.2 19.0 %all-to-all-start.1 = ((bf16[4,4,128,128]{3,2,1,0:T(8,128)(2,1)}), bf16[4,4,128,128]{3,2,1,0:T(8,128)(2,1)S(1)}, u32[]{:S(2)}, u32[]{:S(2)}) async-start(bf16[4,4,128,128]{3,2,1,0:T(8,128)(2,1)} %bitcast.12), calls=%async_computation.1 | async-start | bytes 1048576 | tf_op jit(solution)/shard_map/all_to_all | solution.py:97
  28.2 42.4 %all-gather.2.cloned.1.call-start = ((), (), s32[]{:S(2)}) async-start(), calls=%async_computation.5 | async-start | bytes 2359296 | tf_op jit(solution)/shard_map/all_gather | solution.py:133
  43.6 109.6 %reduce-scatter.5.cloned.1.call-start = ((), (), s32[]{:S(2)}) async-start(), calls=%async_computation.7 | async-start | bytes 2359296 | tf_op jit(solution)/shard_map/reduce_scatter | solution.py:160
  112.0 49.1 %copy-start.6 = (s32[1,16]{1,0:T(1,128)S(1)}, s32[1,16]{1,0:T(1,128)}, u32[]{:S(2)}) copy-start(s32[1,16]{1,0:T(1,128)} %param.17) | copy-start | bytes 196
  154.9 30.6 %copy-start.2 = (f32[2048,128]{1,0:T(8,128)S(1)}, f32[2048,128]{1,0:T(8,128)}, u32[]{:S(2)}) copy-start(f32[2048,128]{1,0:T(8,128)} %copy-done.1) | copy-start | bytes 3145732
  155.8 28.8 %all-to-all-start.2 = ((bf16[4,4,128,128]{3,2,1,0:T(8,128)(2,1)}), bf16[4,4,128,128]{3,2,1,0:T(8,128)(2,1)S(1)}, u32[]{:S(2)}, u32[]{:S(2)}) async-start(bf16[4,4,128,128]{3,2,1,0:T(8,128)(2,1)} %select_select_fusion.2), calls=%async_computation.4 | async-start | bytes 1048576 | tf_op jit(solution)/shard_map/all_to_all | solution.py:165
  160.4 22.9 %reduce-scatter.3.cloned.1.call-start = ((), (), s32[]{:S(2)}) async-start(), calls=%async_computation.6 | async-start | bytes 81920 | tf_op jit(solution)/shard_map/reduce_scatter | solution.py:157
Sparse Core Ops, SparseCore 0:
  43.7 26.8 all-gather.1
  112.1 41.0 reduce-scatter.4
  163.4 19.7 reduce-scatter.2
where the time goes:
time: 196 us
  waiting for transfers between devices  103 us (53%)
  matrix products  25.7 us (13%)
  local copies, waits for them, and re-layouts  25.6 us (13%)
  starting transfers between devices  16.1 us (8%)
  between operations  14 us (7%)
  other arithmetic  10.6 us (5%)
    reduce_scatter x1, waiting for transfers between devices, on_device(): lax.psum_scatter(emb_acc.astype(jnp.bfloat16), 'pb', scatter_dimension=0,...  41.1 us
    all_gather x1, waiting for transfers between devices, on_device(): backward_key_pieces = lax.all_gather(local_emb, 'pb', axis=0, tiled=True)  26.9 us
    reduce_scatter x1, waiting for transfers between devices, on_device(): lax.psum_scatter(query_acc.astype(jnp.bfloat16), 'pa', scatter_dimension=...  22.1 us
    all_to_all x1, waiting for transfers between devices, on_device(): lax.all_to_all(outgoing, 'pa', split_axis=0, concat_axis=0, tiled=True)  12.5 us
    dot_general x8, matrix products, backward_one_shard(): jnp.einsum('rk,rd->kd', coefficient, queries, preferred_element_type=jnp....  8.05 us
    dynamic_slice x8, local copies, waits for them, and re-layouts, forward_one_shard(): key_block = lax.dynamic_slice_in_dim(key_pieces, turn * PD, PD, 0)  7.78 us
    dynamic_slice x8, local copies, waits for them, and re-layouts, backward_one_shard(): key_block = lax.dynamic_slice_in_dim(backward_key_pieces, turn * PD, PD, 0)  7.74 us
    all_to_all x1, starting transfers between devices, on_device(): lax.all_to_all(labels.reshape(width_pa, sendable), 'pa', split_axis=0, co...  6.35 us
  transfers between devices with their start and end apart: 6, of which 4 were waited for; matrix products, arithmetic and copies ran while one was open for 5% of the time, Pallas kernels for 0%

commit v1 on v0

--- a/solution.py
+++ b/solution.py
@@ -14,6 +14,16 @@
 inv_temp = 20.0
 rrf_offset = 60.0
 norm_eps = 1e-06
+
+
+def around_the_ring(x, axis, dim):
+    size = lax.axis_size(axis)
+    held, parts = (x, [x])
+    for _ in range(size - 1):
+        held = lax.ppermute(held, axis, [(i, (i + 1) % size) for i in range(size)])
+        parts.insert(0, held)
+    line = jnp.concatenate(parts, axis=dim)
+    return jnp.roll(line, (lax.axis_index(axis) + 1) * x.shape[dim], axis=dim)
 
 
 def normalize(hid_rows, weight):
@@ -130,7 +140,7 @@
         jnp.zeros((query_rows, DIM), jnp.float32),
         jnp.zeros((passages_all * LEN, DIM), jnp.float32),
     )
-    backward_key_pieces = lax.all_gather(local_emb, "pb", axis=0, tiled=True)
+    backward_key_pieces = around_the_ring(local_emb, "pb", 0)
     shards = backward_key_pieces.shape[0] // PD
 
     def backward_one_shard(turn, state):

time: 196 us -> 221 us (1.13)
  waiting for transfers between devices: 103 us -> 126 us
    ppermute x0 -> x7, waiting for transfers between devices: none -> 51.2 us  [around_the_ring(): held = lax.ppermute(held, axis, [(i, (i + 1) % size) for i in range(size)])]
    all_gather x1, waiting for transfers between devices: 26.9 us -> 0.01 us  [on_device(): key_pieces = lax.all_gather(local_emb, 'pb', axis=0, tiled=True)]
  transfers between devices with their start and end apart: 6 -> 13, of which waited for: 4 -> 10; matrix products, arithmetic and copies ran while one was open for 5% -> 5% of each run, Pallas kernels for 0% -> 0%
where the time goes in v1:
time: 221 us; the launch traced here: 220 us
  waiting for transfers between devices  126 us (57%)
  local copies, waits for them, and re-layouts  27.6 us (12%)
  matrix products  25.8 us (12%)
  starting transfers between devices  16.2 us (7%)
  between operations  14.1 us (6%)
  other arithmetic  10.2 us (5%)
    ppermute x7, waiting for transfers between devices, around_the_ring(): held = lax.ppermute(held, axis, [(i, (i + 1) % size) for i in range(size)])  51.2 us
    reduce_scatter x1, waiting for transfers between devices, on_device(): lax.psum_scatter(emb_acc.astype(jnp.bfloat16), 'pb', scatter_dimension=0,...  39.8 us
    reduce_scatter x1, waiting for transfers between devices, on_device(): lax.psum_scatter(query_acc.astype(jnp.bfloat16), 'pa', scatter_dimension=...  22 us
    all_to_all x1, waiting for transfers between devices, on_device(): lax.all_to_all(outgoing, 'pa', split_axis=0, concat_axis=0, tiled=True)  12.5 us
    dot_general x8, matrix products, backward_one_shard(): jnp.einsum('rk,rd->kd', coefficient, queries, preferred_element_type=jnp....  8.09 us
    dynamic_slice x8, local copies, waits for them, and re-layouts, forward_one_shard(): key_block = lax.dynamic_slice_in_dim(key_pieces, turn * PD, PD, 0)  7.8 us
    dynamic_slice x8, local copies, waits for them, and re-layouts, backward_one_shard(): key_block = lax.dynamic_slice_in_dim(backward_key_pieces, turn * PD, PD, 0)  7.79 us
    all_to_all x1, starting transfers between devices, on_device(): lax.all_to_all(labels.reshape(width_pa, sendable), 'pa', split_axis=0, co...  6.35 us
  transfers between devices with their start and end apart: 13, of which 10 were waited for; matrix products, arithmetic and copies ran while one was open for 5% of the time, Pallas kernels for 0%

profile of v1, /device:TPU:0, one launch (start us, length us, event | category | flops | bytes accessed | tf_op | source)
XLA Modules:
  0.0 220.5 jit_solution(17515156087065264146)
XLA Ops:
  7.2 0.7 fusion.22
  7.9 0.7 fusion.34
  8.7 0.7 fusion.18
  9.6 0.7 select_n.184
  10.3 6.3 %all-to-all-start = ((s32[4,1,4]{2,1,0:T(1,128)}), s32[4,1,4]{2,1,0:T(1,128)S(1)}, u32[]{:S(2)}, u32[]{:S(2)}) async-start(s32[4,1,4]{2,1,0:T(1,128)} %bitcast.9), calls=%async_computation | async-start | bytes 4096 | tf_op jit(solution)/shard_map/all_to_all | solution.py:108
  16.7 3.5 %multiply_reduce_fusion = (f32[2048]{0:T(1024)S(1)}, f32[2048,128]{1,0:T(8,128)S(1)}) fusion(bf16[2048,1024]{1,0:T(8,128)(2,1)} %bitcast.128, bf16[1024,128]{1,0:T(8,128)(2,1)S(1)} %copy-done), kind=kOutput, calls=%fused_computation.31 | convolution fusion | flops 537393152 | bytes 5513216 | tf_op jit(solution)/shard_map/dot_general | solution.py:30
  20.3 0.9 copy-done.1
  21.6 0.6 gather_fusion.2
  22.2 0.9 select_select_fusion.1
  23.1 5.1 %all-to-all-start.1 = ((bf16[4,4,128,128]{3,2,1,0:T(8,128)(2,1)}), bf16[4,4,128,128]{3,2,1,0:T(8,128)(2,1)S(1)}, u32[]{:S(2)}, u32[]{:S(2)}) async-start(bf16[4,4,128,128]{3,2,1,0:T(8,128)(2,1)} %bitcast.12), calls=%async_computation.1 | async-start | bytes 1048576 | tf_op jit(solution)/shard_map/all_to_all | solution.py:107
  28.8 0.7 fusion.23
  29.7 12.5 %all-to-all-done.1 = bf16[4,4,128,128]{3,2,1,0:T(8,128)(2,1)S(1)} async-done(((bf16[4,4,128,128]{3,2,1,0:T(8,128)(2,1)}), bf16[4,4,128,128]{3,2,1,0:T(8,128)(2,1)S(1)}, u32[]{:S(2)}, u32[]{:S(2)}) %all-to-all-start.1) | async-done | bytes 524320 | tf_op jit(solution)/shard_map/all_to_all | solution.py:107
  43.0 6.7 %collective-permute-done = bf16[8,128,128]{2,1,0:T(8,128)(2,1)S(1)} collective-permute-done((bf16[8,128,128]{2,1,0:T(8,128)(2,1)S(1)}, bf16[8,128,128]{2,1,0:T(8,128)(2,1)S(1)}, u32[]{:S(2)}, u32[]{:S(2)}) %collective-permute-start) | collective-permute-done | bytes 262176 | tf_op jit(solution)/shard_map/ppermute | solution.py:23
  49.7 6.6 %collective-permute-done.1 = bf16[8,128,128]{2,1,0:T(8,128)(2,1)S(1)} collective-permute-done((bf16[8,128,128]{2,1,0:T(8,128)(2,1)S(1)}, bf16[8,128,128]{2,1,0:T(8,128)(2,1)S(1)}, u32[]{:S(2)}, u32[]{:S(2)}) %collective-permute-start.1) | collective-permute-done | bytes 262176 | tf_op jit(solution)/shard_map/ppermute | solution.py:23
  56.3 9.5 %collective-permute-done.2 = bf16[8,128,128]{2,1,0:T(8,128)(2,1)S(1)} collective-permute-done((bf16[8,128,128]{2,1,0:T(8,128)(2,1)S(1)}, bf16[8,128,128]{2,1,0:T(8,128)(2,1)S(1)}, u32[]{:S(2)}, u32[]{:S(2)}) %collective-permute-start.2) | collective-permute-done | bytes 262176 | tf_op jit(solution)/shard_map/ppermute | solution.py:23
  65.8 7.3 %collective-permute-done.3 = bf16[8,128,128]{2,1,0:T(8,128)(2,1)S(1)} collective-permute-done((bf16[8,128,128]{2,1,0:T(8,128)(2,1)S(1)}, bf16[8,128,128]{2,1,0:T(8,128)(2,1)S(1)}, u32[]{:S(2)}, u32[]{:S(2)}) %collective-permute-start.3) | collective-permute-done | bytes 262176 | tf_op jit(solution)/shard_map/ppermute | solution.py:23
  73.2 7.8 %collective-permute-done.4 = bf16[8,128,128]{2,1,0:T(8,128)(2,1)S(1)} collective-permute-done((bf16[8,128,128]{2,1,0:T(8,128)(2,1)S(1)}, bf16[8,128,128]{2,1,0:T(8,128)(2,1)S(1)}, u32[]{:S(2)}, u32[]{:S(2)}) %collective-permute-start.4) | collective-permute-done | bytes 262176 | tf_op jit(solution)/shard_map/ppermute | solution.py:23
  80.9 6.7 %collective-permute-done.5 = bf16[8,128,128]{2,1,0:T(8,128)(2,1)S(1)} collective-permute-done((bf16[8,128,128]{2,1,0:T(8,128)(2,1)S(1)}, bf16[8,128,128]{2,1,0:T(8,128)(2,1)S(1)}, u32[]{:S(2)}, u32[]{:S(2)}) %collective-permute-start.5) | collective-permute-done | bytes 262176 | tf_op jit(solution)/shard_map/ppermute | solution.py:23
  87.7 6.7 %collective-permute-done.6 = bf16[8,128,128]{2,1,0:T(8,128)(2,1)S(1)} collective-permute-done((bf16[8,128,128]{2,1,0:T(8,128)(2,1)S(1)}, bf16[8,128,128]{2,1,0:T(8,128)(2,1)S(1)}, u32[]{:S(2)}, u32[]{:S(2)}) %collective-permute-start.6) | collective-permute-done | bytes 262176 | tf_op jit(solution)/shard_map/ppermute | solution.py:23
  95.2 1.5 constant_dynamic-slice_fusion.3
  96.8 12.0 %while.31 = (s32[]{:T(128)}, f32[256,64]{0,1:T(8,128)S(1)}, bf16[64,128,128]{2,1,0:T(8,128)(2,1)}, bf16[256,128]{1,0:T(8,128)(2,1)S(1)}, s32[]{:T(128)}, /*index=5*/s32[]{:T(128)}, s32[]{:T(128)}, s32[]{:T(128)}) while((s32[]{:T(128)}, f32[256,64]{0,1:T(8,128)S(1)}, bf16[64,128,128]{2,1,0:T(8,128)(2,1)}, bf16[256,128]{1,0:T(8,128)(2,1)S(1)}, ...), condition=%wide.region_9.11_spmd, body=%wide.region_6.10_spmd.sunk | while | flops 68155400 | bytes 2998411 | solution.py:126
  96.8 1.0 constant_dynamic-slice_fusion.6
  98.3 1.0 constant_dynamic-slice_fusion.6
  99.8 1.0 constant_dynamic-slice_fusion.6
  101.3 1.0 constant_dynamic-slice_fusion.6
  102.8 1.0 constant_dynamic-slice_fusion.6
  104.3 1.0 constant_dynamic-slice_fusion.6
  105.8 1.0 constant_dynamic-slice_fusion.6
  107.3 1.0 constant_dynamic-slice_fusion.6
  109.0 1.5 broadcast_in_dim.131
  110.5 27.8 %while.32 = (s32[]{:T(128)}, f32[256,128]{1,0:T(8,128)S(1)}, bf16[8192,128]{1,0:T(8,128)(2,1)}, f32[256,64]{0,1:T(8,128)S(1)}, bf16[64,128,128]{2,1,0:T(8,128)(2...) while((s32[]{:T(128)}, f32[256,128]{1,0:T(8,128)S(1)}, ...), condition=%wide.region_12.14_spmd.clone, body=%wide.region_11.13_spmd.clone.sunk | while | flops 203229184 | bytes 7274735 | solution.py:166
  110.5 1.0 constant_dynamic-slice_fusion.7
  111.8 1.0 convolution_dynamic-update-slice_fusion.2
  113.2 0.7 fusion.54
  113.9 1.0 constant_dynamic-slice_fusion.7
  115.3 1.0 convolution_dynamic-update-slice_fusion.2
  116.6 0.7 fusion.54
  117.4 1.0 constant_dynamic-slice_fusion.7
  118.8 1.0 convolution_dynamic-update-slice_fusion.2
  120.1 0.7 fusion.54
  120.9 1.0 constant_dynamic-slice_fusion.7
  122.3 1.0 convolution_dynamic-update-slice_fusion.2
  123.6 0.7 fusion.54
  124.4 1.0 constant_dynamic-slice_fusion.7
  125.7 1.0 convolution_dynamic-update-slice_fusion.2
  127.1 0.7 fusion.54
  127.9 1.0 constant_dynamic-slice_fusion.7
  129.2 1.0 convolution_dynamic-update-slice_fusion.2
  130.6 0.7 fusion.54
  131.3 1.0 constant_dynamic-slice_fusion.7
  132.7 1.0 convolution_dynamic-update-slice_fusion.2
  134.0 0.7 fusion.54
  134.8 1.0 constant_dynamic-slice_fusion.7
  136.2 1.0 convolution_dynamic-update-slice_fusion.2
  137.5 0.7 fusion.54
  138.5 39.8 %reduce-scatter.5.cloned.1.call-done = bf16[1024,128]{1,0:T(8,128)(2,1)} async-done(((bf16[8192,128]{1,0:T(8,128)(2,1)}), bf16[1024,128]{1,0:T(8,128)(2,1)}) %reduce-scatter.5.cloned.1.call-update) | async-done | bytes 262160 | tf_op jit(solution)/shard_map/reduce_scatter | solution.py:170
  178.3 1.6 gather_fusion.1
  179.9 0.9 select_select_fusion.2
  180.8 4.6 %all-to-all-start.2 = ((bf16[4,4,128,128]{3,2,1,0:T(8,128)(2,1)}), bf16[4,4,128,128]{3,2,1,0:T(8,128)(2,1)S(1)}, u32[]{:S(2)}, u32[]{:S(2)}) async-start(bf16[4,4,128,128]{3,2,1,0:T(8,128)(2,1)} %select_select_fusion.2), calls=%async_computation.4 | async-start | bytes 1048576 | tf_op jit(solution)/shard_map/all_to_all | solution.py:175
  186.2 22.0 %reduce-scatter.3.cloned.1.call-done = bf16[64,128]{1,0:T(8,128)(2,1)} async-done(((bf16[256,128]{1,0:T(8,128)(2,1)}), bf16[64,128]{1,0:T(8,128)(2,1)}) %reduce-scatter.3.cloned.1.call-update) | async-done | bytes 16400 | tf_op jit(solution)/shard_map/reduce_scatter | solution.py:167
  208.2 1.3 convert_element_type.66
  209.6 0.6 gather_fusion.3
  210.4 0.7 fusion.8
  211.0 2.9 %convolution_convert_fusion = bf16[2048,1024]{1,0:T(8,128)(2,1)} fusion(bf16[1024,128]{1,0:T(8,128)(2,1)S(1)} %copy-done, bf16[2048,128]{1,0:T(8,128)(2,1)S(1)} %bitcast.129, f32[2048,128]{1,0:T(8,128)S(1)} %copy-done.2, f32[2048]{0:T(1024)S(1)} %fusion.8, f32[2048]{0:T(1024)S(1)} %add_rsqrt_fusion), kind=kOutput, calls=%fused_computation.25 | convolution fusion | flops 540540928 | bytes 6045696 | tf_op jit(solution)/shard_map/rd,hd->rh/dot_general | solution.py:181
  (129 shorter events, 13.8 us)
Async XLA Ops:
  7.2 9.5 %copy-start = (bf16[1024,128]{1,0:T(8,128)(2,1)S(1)}, bf16[1024,128]{1,0:T(8,128)(2,1)}, u32[]{:S(2)}) copy-start(bf16[1024,128]{1,0:T(8,128)(2,1)} %param.14) | copy-start | bytes 786436
  10.3 12.8 %all-to-all-start = ((s32[4,1,4]{2,1,0:T(1,128)}), s32[4,1,4]{2,1,0:T(1,128)S(1)}, u32[]{:S(2)}, u32[]{:S(2)}) async-start(s32[4,1,4]{2,1,0:T(1,128)} %bitcast.9), calls=%async_computation | async-start | bytes 4096 | tf_op jit(solution)/shard_map/all_to_all | solution.py:108
  20.2 1.0 copy-start.1
  20.2 67.4 %copy-start.5 = (s32[8,1,64]{2,1,0:T(1,128)S(1)}, s32[8,1,64]{2,1,0:T(1,128)}, u32[]{:S(2)}) copy-start(s32[8,1,64]{2,1,0:T(1,128)} %param.15) | copy-start | bytes 6148
  20.2 67.4 %copy-start.6 = (s32[8,1,64]{2,1,0:T(1,128)S(1)}, s32[8,1,64]{2,1,0:T(1,128)}, u32[]{:S(2)}) copy-start(s32[8,1,64]{2,1,0:T(1,128)} %param.16) | copy-start | bytes 6148
  23.1 19.0 %all-to-all-start.1 = ((bf16[4,4,128,128]{3,2,1,0:T(8,128)(2,1)}), bf16[4,4,128,128]{3,2,1,0:T(8,128)(2,1)S(1)}, u32[]{:S(2)}, u32[]{:S(2)}) async-start(bf16[4,4,128,128]{3,2,1,0:T(8,128)(2,1)} %bitcast.12), calls=%async_computation.1 | async-start | bytes 1048576 | tf_op jit(solution)/shard_map/all_to_all | solution.py:107
  28.2 68.5 %all-gather.2.cloned.1.call-start = ((), (), s32[]{:S(2)}) async-start(), calls=%async_computation.5 | async-start | bytes 2359296 | tf_op jit(solution)/shard_map/all_gather | solution.py:117
  42.9 6.8 %copy-start.4 = (bf16[8,128,128]{2,1,0:T(8,128)(2,1)}, bf16[8,128,128]{2,1,0:T(8,128)(2,1)S(1)}, u32[]{:S(2)}) copy-start(bf16[8,128,128]{2,1,0:T(8,128)(2,1)S(1)} %broadcast_select_fusion) | copy-start | bytes 786436
  42.9 6.7 %collective-permute-start = (bf16[8,128,128]{2,1,0:T(8,128)(2,1)S(1)}, bf16[8,128,128]{2,1,0:T(8,128)(2,1)S(1)}, u32[]{:S(2)}, u32[]{:S(2)}) collective-permute-start(bf16[8,128,128]{2,1,0:T(8,128)(2,1)S(1)} %broadcast_select_fusion), channel_id=1, source_target_pairs={{0,4},{4,8},{8,12},{12,16},{16,20},{20,24},{24,28},{28,0},{1,5},{5... | collective-permute-start | bytes 786440 | tf_op jit(solution)/shard_map/ppermute | solution.py:23
  49.6 6.7 %collective-permute-start.1 = (bf16[8,128,128]{2,1,0:T(8,128)(2,1)S(1)}, bf16[8,128,128]{2,1,0:T(8,128)(2,1)S(1)}, u32[]{:S(2)}, u32[]{:S(2)}) collective-permute-start(bf16[8,128,128]{2,1,0:T(8,128)(2,1)S(1)} %collective-permute-done), channel_id=1, source_target_pairs={{0,4},{4,8},{8,12},{12,16},{16,20},{20,24},{24,28},{28,0},{1,5},{5... | collective-permute-start | bytes 786440 | tf_op jit(solution)/shard_map/ppermute | solution.py:23
  49.7 128.6 %reduce-scatter.5.cloned.1.call-start = ((), (), s32[]{:S(2)}) async-start(), calls=%async_computation.7 | async-start | bytes 2359296 | tf_op jit(solution)/shard_map/reduce_scatter | solution.py:170
  56.3 9.5 %collective-permute-start.2 = (bf16[8,128,128]{2,1,0:T(8,128)(2,1)S(1)}, bf16[8,128,128]{2,1,0:T(8,128)(2,1)S(1)}, u32[]{:S(2)}, u32[]{:S(2)}) collective-permute-start(bf16[8,128,128]{2,1,0:T(8,128)(2,1)S(1)} %collective-permute-done.1), channel_id=1, source_target_pairs={{0,4},{4,8},{8,12},{12,16},{16,20},{20,24},{24,28},{28,0},{1,5},{5... | collective-permute-start | bytes 786440 | tf_op jit(solution)/shard_map/ppermute | solution.py:23
  65.8 7.3 %collective-permute-start.3 = (bf16[8,128,128]{2,1,0:T(8,128)(2,1)S(1)}, bf16[8,128,128]{2,1,0:T(8,128)(2,1)S(1)}, u32[]{:S(2)}, u32[]{:S(2)}) collective-permute-start(bf16[8,128,128]{2,1,0:T(8,128)(2,1)S(1)} %collective-permute-done.2), channel_id=1, source_target_pairs={{0,4},{4,8},{8,12},{12,16},{16,20},{20,24},{24,28},{28,0},{1,5},{5... | collective-permute-start | bytes 786440 | tf_op jit(solution)/shard_map/ppermute | solution.py:23
  73.2 7.8 %collective-permute-start.4 = (bf16[8,128,128]{2,1,0:T(8,128)(2,1)S(1)}, bf16[8,128,128]{2,1,0:T(8,128)(2,1)S(1)}, u32[]{:S(2)}, u32[]{:S(2)}) collective-permute-start(bf16[8,128,128]{2,1,0:T(8,128)(2,1)S(1)} %collective-permute-done.3), channel_id=1, source_target_pairs={{0,4},{4,8},{8,12},{12,16},{16,20},{20,24},{24,28},{28,0},{1,5},{5... | collective-permute-start | bytes 786440 | tf_op jit(solution)/shard_map/ppermute | solution.py:23
  80.9 6.7 %collective-permute-start.5 = (bf16[8,128,128]{2,1,0:T(8,128)(2,1)S(1)}, bf16[8,128,128]{2,1,0:T(8,128)(2,1)S(1)}, u32[]{:S(2)}, u32[]{:S(2)}) collective-permute-start(bf16[8,128,128]{2,1,0:T(8,128)(2,1)S(1)} %collective-permute-done.4), channel_id=1, source_target_pairs={{0,4},{4,8},{8,12},{12,16},{16,20},{20,24},{24,28},{28,0},{1,5},{5... | collective-permute-start | bytes 786440 | tf_op jit(solution)/shard_map/ppermute | solution.py:23
  87.6 6.7 %collective-permute-start.6 = (bf16[8,128,128]{2,1,0:T(8,128)(2,1)S(1)}, bf16[8,128,128]{2,1,0:T(8,128)(2,1)S(1)}, u32[]{:S(2)}, u32[]{:S(2)}) collective-permute-start(bf16[8,128,128]{2,1,0:T(8,128)(2,1)S(1)} %collective-permute-done.5), channel_id=1, source_target_pairs={{0,4},{4,8},{8,12},{12,16},{16,20},{20,24},{24,28},{28,0},{1,5},{5... | collective-permute-start | bytes 786440 | tf_op jit(solution)/shard_map/ppermute | solution.py:23
  94.8 2.0 copy-start.3
  138.3 47.9 %copy-start.7 = (s32[1,16]{1,0:T(1,128)S(1)}, s32[1,16]{1,0:T(1,128)}, u32[]{:S(2)}) copy-start(s32[1,16]{1,0:T(1,128)} %param.17) | copy-start | bytes 196
  138.3 72.1 %copy-start.2 = (f32[2048,128]{1,0:T(8,128)S(1)}, f32[2048,128]{1,0:T(8,128)}, u32[]{:S(2)}) copy-start(f32[2048,128]{1,0:T(8,128)} %copy-done.1) | copy-start | bytes 3145732
  180.8 28.8 %all-to-all-start.2 = ((bf16[4,4,128,128]{3,2,1,0:T(8,128)(2,1)}), bf16[4,4,128,128]{3,2,1,0:T(8,128)(2,1)S(1)}, u32[]{:S(2)}, u32[]{:S(2)}) async-start(bf16[4,4,128,128]{3,2,1,0:T(8,128)(2,1)} %select_select_fusion.2), calls=%async_computation.4 | async-start | bytes 1048576 | tf_op jit(solution)/shard_map/all_to_all | solution.py:175
  185.4 22.8 %reduce-scatter.3.cloned.1.call-start = ((), (), s32[]{:S(2)}) async-start(), calls=%async_computation.6 | async-start | bytes 81920 | tf_op jit(solution)/shard_map/reduce_scatter | solution.py:167
Sparse Core Ops, SparseCore 0:
  49.8 30.4 all-gather.1
  138.5 39.7 reduce-scatter.4
  188.4 19.7 reduce-scatter.2
